TPU v7x, 128 devices: a whole 4x4x4 slice. The times are simulated.
128 devices in a mesh: space: 32 (over y, z, core), tm: 4 (over x).
Axes of the slice: x: 4, y: 4, z: 4, core: 2. Of those that a mesh axis runs over, the one named last changes fastest.
Arguments:
- field: float32 [32768, 8192], P('space', 'tm'), may hold values from -6 to 6
- range_test: float32 [8192, 256], P('tm'), may hold values from -0.0625 to 0.0625
- corange_test: float32 [512, 32768], P(None, 'space'), may hold values from -0.03125 to 0.03125
Outputs:
- left_factor: float32 [32768, 256], P('space')
- right_factor: float32 [256, 8192], P(None, 'tm')
- residual: float32 [32768, 8192], P('space', 'tm')
All inputs are finite; a program needn't handle non-finite values.
Results may differ from a plain program's by a relative error of at most 0.00017.
Values sent between devices are 32-bit elements; how exact they have to be, the bound alone decides.
A program may use at most 128 MiB of HBM per device.

v0:
```python
import functools

import jax
import jax.numpy as jnp
from jax import lax
from jax.experimental import pallas as pl
from jax.experimental.pallas import tpu as pltpu
from jax.sharding import PartitionSpec as P

MESH = pl.DeviceIdType.MESH
F32, BF16 = jnp.float32, jnp.bfloat16
HI = lax.Precision.HIGHEST


def halves(x):
    high = x.astype(BF16)
    return high, (x - high.astype(F32)).astype(BF16)


def mm(a, b):
    return jnp.dot(a, b, preferred_element_type=F32)


def mm3(ah, al, bh, bl):
    return mm(ah, bh) + (mm(ah, bl) + mm(al, bh))


def exact(a, b):
    return jnp.dot(a, b, preferred_element_type=F32, precision=HI)


def eliminate(matrix):
    lane = lax.broadcasted_iota(jnp.int32, (8, 128), 1)
    sub = lax.broadcasted_iota(jnp.int32, (8, 128), 0)

    def group(g, blocks):
        old = blocks
        blocks = list(blocks)
        for i in range(8):
            at = lane == i
            pivot = blocks[0]
            col = jnp.broadcast_to(pivot[:, i : i + 1], (8, 128))
            inv = 1.0 / jnp.broadcast_to(col[i : i + 1, :], (8, 128))
            row = jnp.broadcast_to(pivot[i : i + 1, :], (8, 128))
            row = jnp.where(at, 1.0, row) * inv
            below = sub > i
            blocks[0] = jnp.where(below, jnp.where(at, 0.0, pivot) - col * row, pivot)
            for b in range(1, 16):
                blk = blocks[b]
                c = jnp.broadcast_to(blk[:, i : i + 1], (8, 128))
                blocks[b] = jnp.where(at, 0.0, blk) - c * row
        for b in range(1, 16):
            blocks[b] = jnp.where(b < 16 - g, blocks[b], old[b])
        blocks = [pltpu.roll(x, 120, 1) for x in blocks]
        return tuple(blocks[1:] + blocks[:1])

    blocks = tuple(matrix[8 * b : 8 * b + 8, :] for b in range(16))
    blocks = lax.fori_loop(0, 16, group, blocks)
    full = jnp.concatenate(blocks, axis=0)
    r = lax.broadcasted_iota(jnp.int32, (128, 128), 0)
    c = lax.broadcasted_iota(jnp.int32, (128, 128), 1)
    diag = jnp.sum(jnp.where(r == c, full, 0.0), axis=1, keepdims=True)
    scale = 1.0 / jnp.sqrt(diag)
    upper = jnp.where(c >= r, full, 0.0) * scale
    lower = jnp.where(c < r, full, jnp.where(c == r, 1.0, 0.0)) * scale
    return upper, lower


def kernel(
    field, rng, cor, s_out, x_out, j_out, r_out,
    fbuf, rbuf, obuf, fh, fl, rh, rl, oh, ol,
    part, precv, sbuf,
    cpart, crecv, c1a, c1b, h2a, h2b, c2a, c2b, cfin,
    m_part, m_r0, m_h1, m_r1, m_h2, m_r2, m_r3, m_fin,
    g_part, g_r0, g_h1, g_r1, g_h2, g_r2, g_r3, g_fin,
    xbuf, jbuf, rfac,
    lsem, ssem, rsem, csend, crecvs,
):
    x = lax.axis_index("tm")
    sp = lax.axis_index("space")
    core = lax.rem(sp, 2)
    z = lax.rem(sp // 2, 4)
    y = sp // 8
    oc = 1 - core

    def plus(v, d):
        return lax.rem(v + d, 4)

    def to_core():
        return {"space": sp + 1 - 2 * core}

    def to_z(zz):
        return {"space": y * 8 + zz * 2 + core}

    def to_y(yy):
        return {"space": yy * 8 + z * 2 + core}

    def to_x(xx):
        return {"tm": xx}

    def al(v, n):
        return pl.multiple_of(v, n)

    count = [0]
    sent = []

    def send(src, dst, peer):
        i = count[0]
        count[0] += 1
        copy = pltpu.make_async_remote_copy(
            src_ref=src, dst_ref=dst, send_sem=ssem.at[i], recv_sem=rsem.at[i],
            device_id=peer, device_id_type=MESH)
        copy.start()
        sent.append(copy)
        return copy

    loads = [pltpu.make_async_copy(rng, rbuf, lsem.at[0])]
    order = (2, 1, 3, 0)
    for n, d in enumerate(order):
        rows = pl.ds(al(plus(x, d) * 256, 256), 256)
        loads.append(pltpu.make_async_copy(field.at[rows], fbuf.at[rows], lsem.at[1 + n]))
    loads.append(pltpu.make_async_copy(cor, obuf, lsem.at[5]))
    for load in loads:
        load.start()

    barrier = pltpu.get_barrier_semaphore()
    peers = [to_core()]
    for d in (1, 2, 3):
        peers += [to_z(plus(z, d)), to_y(plus(y, d)), to_x(plus(x, d))]
    for peer in peers:
        pl.semaphore_signal(barrier, inc=1, device_id=peer, device_id_type=MESH)
    pl.semaphore_wait(barrier, len(peers))

    def all_reduce(w, part, r0, h1, r1, h2, r2, r3, fin):
        base = al(core * 256, 256)
        cp = send(part.at[pl.ds(al(oc * 256, 256), 256)], r0, to_core())
        yield
        cp.wait_recv()
        h1[...] = part[pl.ds(base, 256), :] + r0[...]
        cps = []
        for d in (1, 2, 3):
            zz, yy = plus(z, d), plus(y, d)
            cps.append(send(h1.at[pl.ds(al(32 * zz, 32), 32)], r1.at[0, d - 1], to_z(zz)))
            cps.append(send(h1.at[pl.ds(al(128 + 32 * yy, 32), 32)], r1.at[1, d - 1], to_y(yy)))
        yield
        for cp in cps:
            cp.wait_recv()
        for k, v in ((0, z), (1, y)):
            h2[k] = (h1[pl.ds(al(128 * k + 32 * v, 32), 32), :] + r1[k, 0]) + (r1[k, 1] + r1[k, 2])
        cps = []
        for d in (1, 2, 3):
            zz, yy = plus(z, d), plus(y, d)
            cps.append(send(h2.at[0, pl.ds(al(8 * yy, 8), 8)], r2.at[0, d - 1], to_y(yy)))
            cps.append(send(h2.at[1, pl.ds(al(8 * zz, 8), 8)], r2.at[1, d - 1], to_z(zz)))
        yield
        for cp in cps:
            cp.wait_recv()
        for k, v in ((0, y), (1, z)):
            r3[x, 8 * k : 8 * k + 8, :] = (h2[k, pl.ds(al(8 * v, 8), 8), :] + r2[k, 0]) + (r2[k, 1] + r2[k, 2])
        cps = [send(r3.at[x], r3.at[x], to_x(plus(x, d))) for d in (1, 2, 3)]
        yield
        for cp in cps:
            cp.wait_recv()
        total = (r3[0] + r3[1]) + (r3[2] + r3[3])
        a = al(base + 32 * z, 32)
        b = al(base + 128 + 32 * y, 32)
        a8 = pl.ds(al(a + 8 * y, 8), 8)
        b8 = pl.ds(al(b + 8 * z, 8), 8)
        fin[a8, :] = total[0:8]
        fin[b8, :] = total[8:16]
        cps = []
        for d in (1, 2, 3):
            cps.append(send(fin.at[a8], fin.at[a8], to_y(plus(y, d))))
            cps.append(send(fin.at[b8], fin.at[b8], to_z(plus(z, d))))
        yield
        for cp in cps:
            cp.wait_recv()
        a32, b32 = pl.ds(a, 32), pl.ds(b, 32)
        cps = []
        for d in (1, 2, 3):
            cps.append(send(fin.at[a32], fin.at[a32], to_z(plus(z, d))))
            cps.append(send(fin.at[b32], fin.at[b32], to_y(plus(y, d))))
        yield
        for cp in cps:
            cp.wait_recv()
        mine = pl.ds(base, 256)
        cp = send(fin.at[mine], fin.at[mine], to_core())
        yield
        cp.wait_recv()
        yield

    loads[0].wait()
    high, low = halves(rbuf[...])
    rh[...] = high
    rl[...] = low
    pcopies = []
    for n, d in enumerate(order):
        loads[1 + n].wait()
        xx = plus(x, d)
        rows = pl.ds(al(xx * 256, 256), 256)
        high, low = halves(fbuf[rows, :])
        fh[rows, :] = high
        fl[rows, :] = low
        part[rows, :] = mm3(fh[rows, :], fl[rows, :], rh[...], rl[...])
        if d:
            pcopies.append(send(part.at[rows], precv.at[d - 1], to_x(xx)))

    loads[5].wait()
    high, low = halves(obuf[...])
    oh[...] = high
    ol[...] = low
    high, low = halves(part[...])
    m_part[...] = mm3(oh[...], ol[...], high, low)
    ar_m = all_reduce(256, m_part, m_r0, m_h1, m_r1, m_h2, m_r2, m_r3, m_fin)
    next(ar_m)

    other = pl.ds(al(oc * 256, 256), 256)
    mine = pl.ds(al(core * 256, 256), 256)

    def core_copy(j):
        yy, zz = j // 2, lax.rem(j, 2) * 2
        pair = pl.ds(zz, 2)
        return pltpu.make_async_remote_copy(
            src_ref=cpart.at[yy, pair, other], dst_ref=crecv.at[yy, pair],
            send_sem=csend.at[j], recv_sem=crecvs.at[j], device_id=to_core(), device_id_type=MESH)

    def cos_step(j, carry):
        cols = pl.ds(al(j * 256, 256), 256)
        block = mm3(oh[...], ol[...], fh[:, cols], fl[:, cols])
        yy, zz = j // 2, lax.rem(j, 2) * 2
        cpart[yy, zz] = block[:, :128]
        cpart[yy, zz + 1] = block[:, 128:]
        core_copy(j).start()
        return carry

    def cos_join(j, carry):
        core_copy(j).wait_recv()
        yy, zz = j // 2, lax.rem(j, 2) * 2
        pair = pl.ds(zz, 2)
        crecv[yy, pair] = crecv[yy, pair] + cpart[yy, pair, mine]
        return carry

    lax.fori_loop(0, 2, cos_step, 0)
    next(ar_m)
    lax.fori_loop(2, 4, cos_step, 0)
    next(ar_m)
    lax.fori_loop(4, 6, cos_step, 0)
    next(ar_m)
    for cp in pcopies:
        cp.wait_recv()
    own = pl.ds(al(x * 256, 256), 256)
    rows_sum = (part[own, :] + precv[0]) + (precv[1] + precv[2])
    sbuf[own, :] = rows_sum
    scopies = [send(sbuf.at[own], sbuf.at[own], to_x(plus(x, d))) for d in (1, 2, 3)]
    gram = exact(rows_sum.T, rows_sum)
    g_part[0:256, :] = gram[:, :128]
    g_part[256:512, :] = gram[:, 128:]
    ar_g = all_reduce(128, g_part, g_r0, g_h1, g_r1, g_h2, g_r2, g_r3, g_fin)
    next(ar_g)
    next(ar_m)
    lax.fori_loop(6, 8, cos_step, 0)
    next(ar_g)
    next(ar_m)
    lax.fori_loop(0, 8, cos_join, 0)
    c1 = []
    for d in (1, 2, 3):
        zz, yy = plus(z, d), plus(y, d)
        c1.append(send(crecv.at[:, zz, 0:128], c1a.at[d - 1], to_z(zz)))
        c1.append(send(crecv.at[yy, :, 128:256], c1b.at[d - 1], to_y(yy)))
    next(ar_g)
    next(ar_m)
    next(ar_m)
    mixed = m_fin[...]
    mixed_t = mixed.T
    normal = exact(mixed_t, mixed)

    def factor_first(a):
        up, lo = eliminate(a[:128, :128])
        off = exact(lo, a[:128, 128:])
        return up, lo, off, a[128:, 128:] - exact(off.T, off)

    def factor_second(up, lo, off, rest):
        up2, lo2 = eliminate(rest)
        corner = -exact(lo2, exact(off.T, lo))
        zero = jnp.zeros((128, 128), F32)
        left = jnp.concatenate([lo, corner], axis=0)
        right = jnp.concatenate([zero, lo2], axis=0)
        inv = jnp.concatenate([left, right], axis=1)
        top = jnp.concatenate([up, off], axis=1)
        bottom = jnp.concatenate([zero, up2], axis=1)
        return inv, jnp.concatenate([top, bottom], axis=0)

    next(ar_g)
    first = factor_first(normal)
    next(ar_g)
    for cp in c1:
        cp.wait_recv()
    for n in range(4):
        h2a[n] = (crecv[n, z, 0:128, :] + c1a[0, n]) + (c1a[1, n] + c1a[2, n])
        h2b[n] = (crecv[y, n, 128:256, :] + c1b[0, n]) + (c1b[1, n] + c1b[2, n])
    c2 = []
    for d in (1, 2, 3):
        zz, yy = plus(z, d), plus(y, d)
        c2.append(send(h2a.at[yy], c2a.at[d - 1], to_y(yy)))
        c2.append(send(h2b.at[zz], c2b.at[d - 1], to_z(zz)))
    inverse, unused = factor_second(*first)
    next(ar_g)
    for cp in c2:
        cp.wait_recv()
    cbase = al(core * 256, 256)
    cfin[pl.ds(cbase, 128), :] = (h2a[y] + c2a[0]) + (c2a[1] + c2a[2])
    cfin[pl.ds(al(cbase + 128, 128), 128), :] = (h2b[z] + c2b[0]) + (c2b[1] + c2b[2])
    cc = send(cfin.at[mine], cfin.at[mine], to_core())
    solve = exact(inverse.T, exact(inverse, mixed_t))
    cc.wait_recv()
    block = exact(solve, cfin[...])
    half = al(core * 128, 128)
    jbuf[...] = block
    ra = pl.ds(half, 64)
    rb = pl.ds(al(half + 64, 64), 64)
    xbuf[y, z, ra] = jbuf[ra, :]
    xbuf[y, z, rb] = jbuf[rb, :]
    x1 = []
    for d in (1, 2, 3):
        x1.append(send(xbuf.at[y, z, ra], xbuf.at[y, z, ra], to_z(plus(z, d))))
        x1.append(send(xbuf.at[y, z, rb], xbuf.at[y, z, rb], to_y(plus(y, d))))
    next(ar_g)
    next(ar_g)
    for cp in scopies:
        cp.wait_recv()
    outs = [pltpu.make_async_copy(sbuf, s_out, lsem.at[6])]
    outs[0].start()
    gram = jnp.concatenate([g_fin[0:256, :], g_fin[256:512, :]], axis=1)
    for cp in x1:
        cp.wait_recv()
    x2, forward = [], []
    for d in (1, 2, 3):
        x2.append(send(xbuf.at[y, :, ra], xbuf.at[y, :, ra], to_y(plus(y, d))))
        x2.append(send(xbuf.at[:, z, rb], xbuf.at[:, z, rb], to_z(plus(z, d))))
    forward.append(send(xbuf.at[y, :, ra], xbuf.at[y, :, ra], to_core()))
    forward.append(send(xbuf.at[:, z, rb], xbuf.at[:, z, rb], to_core()))
    first = factor_first(gram)
    for d, (ca, cb) in zip((1, 2, 3), zip(x2[0::2], x2[1::2])):
        ca.wait_recv()
        cb.wait_recv()
        yy, zz = plus(y, 4 - d), plus(z, 4 - d)
        forward.append(send(xbuf.at[yy, :, ra], xbuf.at[yy, :, ra], to_core()))
        forward.append(send(xbuf.at[:, zz, rb], xbuf.at[:, zz, rb], to_core()))
    inverse, upper = factor_second(*first)
    jbuf2, rfac2 = jbuf, rfac
    rfac2[0] = inverse
    rfac2[1] = upper
    for cp in forward:
        cp.wait_recv()
    outs.append(pltpu.make_async_copy(xbuf, x_out, lsem.at[7]))
    outs.append(pltpu.make_async_copy(rfac.at[0], j_out, lsem.at[8]))
    outs.append(pltpu.make_async_copy(rfac.at[1], r_out, lsem.at[9]))
    for copy in outs[1:]:
        copy.start()
    for cp in sent:
        cp.wait_send()

    def drain(j, carry):
        core_copy(j).wait_send()
        return carry

    lax.fori_loop(0, 8, drain, 0)
    for copy in outs:
        copy.wait()


def last(scale, field, s, xb, inv, up, left, right, residual, sh, sl):
    @pl.when(pl.program_id(0) == 0)
    def _():
        high, low = halves(s[...])
        sh[...] = high
        sl[...] = low

    j = pl.program_id(0)
    block = jnp.concatenate([xb[0], xb[1]], axis=1)
    xh, xl = halves(block)
    residual[...] = field[...] - mm3(sh[...], sl[...], xh, xl)
    uh, ul = halves(up[...])
    right[...] = mm3(uh, ul, xh, xl)
    ih, il = halves(inv[...].T)
    rows = pl.ds(pl.multiple_of(j * 128, 128), 128)
    left[...] = mm3(sh[rows, :], sl[rows, :], ih, il) * scale


def per_device(cells, field, range_test, corange_test):
    def vm(*shape, dtype=F32):
        return pltpu.VMEM(shape, dtype)

    def reduce_buffers(w):
        return [
            vm(512, w), vm(256, w), vm(256, w), vm(2, 3, 32, w), vm(2, 32, w),
            vm(2, 3, 8, w), vm(4, 16, w), vm(512, w),
        ]

    any_space = pl.BlockSpec(memory_space=pl.ANY)
    s, xb, inv, up = pl.pallas_call(
        kernel,
        out_shape=(
            jax.ShapeDtypeStruct((1024, 256), F32),
            jax.ShapeDtypeStruct((4, 4, 256, 128), F32),
            jax.ShapeDtypeStruct((256, 256), F32),
            jax.ShapeDtypeStruct((256, 256), F32),
        ),
        in_specs=[any_space] * 3,
        out_specs=[any_space] * 4,
        scratch_shapes=[
            vm(1024, 2048), vm(2048, 256), vm(512, 1024),
            vm(1024, 2048, dtype=BF16), vm(1024, 2048, dtype=BF16),
            vm(2048, 256, dtype=BF16), vm(2048, 256, dtype=BF16),
            vm(512, 1024, dtype=BF16), vm(512, 1024, dtype=BF16),
            vm(1024, 256), vm(3, 256, 256), vm(1024, 256),
            vm(4, 4, 512, 128), vm(4, 4, 256, 128),
            vm(3, 4, 128, 128), vm(3, 4, 128, 128), vm(4, 128, 128), vm(4, 128, 128),
            vm(3, 128, 128), vm(3, 128, 128), vm(512, 128),
            *reduce_buffers(256),
            *reduce_buffers(128),
            vm(4, 4, 256, 128), vm(256, 128), vm(2, 256, 256),
            pltpu.SemaphoreType.DMA((10,)),
            pltpu.SemaphoreType.DMA((120,)),
            pltpu.SemaphoreType.DMA((120,)),
            pltpu.SemaphoreType.DMA((8,)),
            pltpu.SemaphoreType.DMA((8,)),
        ],
        compiler_params=pltpu.CompilerParams(
            collective_id=0, has_side_effects=True, vmem_limit_bytes=64 * 1024 * 1024 - 65536),
        name="sketch",
    )(field, range_test, corange_test)
    xb = xb.reshape(16, 256, 128)
    return pl.pallas_call(
        functools.partial(last, float(cells) ** 0.5),
        grid=(8,),
        out_shape=(
            jax.ShapeDtypeStruct((1024, 256), F32),
            jax.ShapeDtypeStruct((256, 2048), F32),
            jax.ShapeDtypeStruct((1024, 2048), F32),
        ),
        in_specs=[
            pl.BlockSpec((1024, 256), lambda j: (0, j)),
            pl.BlockSpec((1024, 256), lambda j: (0, 0)),
            pl.BlockSpec((2, 256, 128), lambda j: (j, 0, 0)),
            pl.BlockSpec((256, 256), lambda j: (0, 0)),
            pl.BlockSpec((256, 256), lambda j: (0, 0)),
        ],
        out_specs=(
            pl.BlockSpec((128, 256), lambda j: (j, 0)),
            pl.BlockSpec((256, 256), lambda j: (0, j)),
            pl.BlockSpec((1024, 256), lambda j: (0, j)),
        ),
        scratch_shapes=[vm(1024, 256, dtype=BF16), vm(1024, 256, dtype=BF16)],
        name="finish",
    )(field, s, xb, inv, up)


def solution(mesh):
    cells = 1024 * mesh.shape["space"]
    return jax.shard_map(
        functools.partial(per_device, cells),
        mesh=mesh,
        in_specs=(P("space", "tm"), P("tm", None), P(None, "space")),
        out_specs=(P("space", None), P(None, "tm"), P("space", "tm")),
        check_vma=False,
    )
```

profile of v0, /device:TPU:1, one launch (start us, length us, event | category | flops | bytes accessed | tf_op | source)
XLA Modules:
  0.0 138.0 jit_solution(3699852351328316550)
XLA Ops:
  0.6 124.4 %sketch.1 = (f32[1024,256]{1,0:T(8,128)}, f32[4,4,256,128]{3,2,1,0:T(8,128)}, f32[256,256]{1,0:T(8,128)}, f32[256,256]{1,0:T(8,128)}) custom-call(f32[1024,2048]{1,0:T(8,128)} %field.3, f32[2048,256]{1,0:T(8,128)} %rng.1, f32[512,1024]{1,0:T(8,128)} %cor.1), custom_call_target="tpu_custom_call" | custom-call | tf_op jit(solution)/shard_map/sketch/pallas_call | solution.py:401
  125.1 13.0 %finish.1 = (f32[1024,256]{1,0:T(8,128)}, f32[256,2048]{1,0:T(8,128)}, f32[1024,2048]{1,0:T(8,128)}) custom-call(f32[1024,2048]{1,0:T(8,128)} %field.3, f32[1024,256]{1,0:T(8,128)} %get-tuple-element.7.s, f32[16,256,128]{2,1,0:T(8,128)} %bitcast.1, f32[256,256]{1,0:T(8,128)} %get-tuple-element.9.inv, f32[256,256]{1,0:T(8,128)} %get-tuple-element.10.up), custom_call_target="tpu_custom_call" | custom-call | tf_op jit(solution)/shard_map/finish/pallas_call | solution.py:434
where the time goes:
time: 138 us
  Pallas kernels  137 us (99%)
    pallas_call x1, Pallas kernels, per_device(): pl.pallas_call(kernel, out_shape=(jax.ShapeDtypeStruct((1024, 256), F32),...  124 us
    pallas_call x1, Pallas kernels, per_device(): pl.pallas_call(functools.partial(last, float(cells) ** 0.5), grid=(8,), o...  13 us

commit v1 on v0

--- a/solution.py
+++ b/solution.py
@@ -33,30 +33,53 @@
     lane = lax.broadcasted_iota(jnp.int32, (8, 128), 1)
     sub = lax.broadcasted_iota(jnp.int32, (8, 128), 0)
 
-    def group(g, blocks):
-        old = blocks
-        blocks = list(blocks)
+    def spread(v, index):
+        return jnp.take_along_axis(v, index, axis=1, mode="promise_in_bounds")
+
+    def level(v, i):
+        return jnp.broadcast_to(v[i : i + 1, :], (8, 128))
+
+    def tree(terms):
+        while len(terms) > 1:
+            terms = [terms[k] + terms[k + 1] for k in range(0, len(terms), 2)]
+        return terms[0]
+
+    def group(active, g, carry):
+        before, *blocks = carry
+        index = [jnp.full((8, 128), 8 * g + i, jnp.int32) for i in range(8)]
+        past = [jnp.maximum(v - 8, 0) for v in index]
+        inside_past = (lane >= 8 * g - 8) & (lane < 8 * g)
+        inside = (lane >= 8 * g) & (lane < 8 * g + 8)
+        w = kept = blocks[0]
+        cols = [spread(w, k) for k in index]
+        old_rows = [level(before, i) for i in range(8)]
+        out = {b: jnp.where(inside_past, 0.0, blocks[b]) for b in range(1, active + 1)}
+        first = [spread(blocks[1], past[i]) * old_rows[i] for i in range(8)]
+        out[1] = out[1] - tree(first)
+        ahead = [spread(out[1], k) for k in index]
         for i in range(8):
-            at = lane == i
-            pivot = blocks[0]
-            col = jnp.broadcast_to(pivot[:, i : i + 1], (8, 128))
-            inv = 1.0 / jnp.broadcast_to(col[i : i + 1, :], (8, 128))
-            row = jnp.broadcast_to(pivot[i : i + 1, :], (8, 128))
-            row = jnp.where(at, 1.0, row) * inv
-            below = sub > i
-            blocks[0] = jnp.where(below, jnp.where(at, 0.0, pivot) - col * row, pivot)
-            for b in range(1, 16):
-                blk = blocks[b]
-                c = jnp.broadcast_to(blk[:, i : i + 1], (8, 128))
-                blocks[b] = jnp.where(at, 0.0, blk) - c * row
-        for b in range(1, 16):
-            blocks[b] = jnp.where(b < 16 - g, blocks[b], old[b])
-        blocks = [pltpu.roll(x, 120, 1) for x in blocks]
-        return tuple(blocks[1:] + blocks[:1])
-
-    blocks = tuple(matrix[8 * b : 8 * b + 8, :] for b in range(16))
-    blocks = lax.fori_loop(0, 16, group, blocks)
-    full = jnp.concatenate(blocks, axis=0)
+            at = lane == index[i]
+            inv = 1.0 / level(cols[i], i)
+            row = jnp.where(at, 1.0, level(w, i))
+            mine = sub == i
+            kept = jnp.where(mine, w, kept)
+            w = jnp.where(mine, row * inv, jnp.where(at, 0.0, w) - (cols[i] * row) * inv)
+            for m in range(i + 1, 8):
+                r = level(cols[m], i)
+                cols[m] = jnp.where(mine, r * inv, cols[m] - (cols[i] * r) * inv)
+            for b in range(2, active + 1):
+                out[b] = out[b] - spread(blocks[b], past[i]) * old_rows[i]
+        new = list(blocks)
+        for b in range(2, active + 1):
+            new[b] = jnp.where(b < 16 - g, out[b], blocks[b])
+        pivot = jnp.where(inside, 0.0, out[1]) - tree([ahead[i] * level(w, i) for i in range(8)])
+        new[1] = jnp.where(g < 15, pivot, blocks[1])
+        return (w, *new[1:], kept)
+
+    carry = (jnp.zeros((8, 128), F32), *(matrix[8 * b : 8 * b + 8, :] for b in range(16)))
+    for n, active in enumerate((15, 11, 7, 3)):
+        carry = lax.fori_loop(4 * n, 4 * n + 4, functools.partial(group, active), carry)
+    full = jnp.concatenate(carry[1:], axis=0)
     r = lax.broadcasted_iota(jnp.int32, (128, 128), 0)
     c = lax.broadcasted_iota(jnp.int32, (128, 128), 1)
     diag = jnp.sum(jnp.where(r == c, full, 0.0), axis=1, keepdims=True)
@@ -67,13 +90,13 @@
 
 
 def kernel(
-    field, rng, cor, s_out, x_out, j_out, r_out,
-    fbuf, rbuf, obuf, fh, fl, rh, rl, oh, ol,
-    part, precv, sbuf,
+    field, rng, cor, fbuf, sbuf, xbuf, j_out, r_out,
+    rbuf, obuf, fh, fl, rh, rl, oh, ol,
+    part, precv,
     cpart, crecv, c1a, c1b, h2a, h2b, c2a, c2b, cfin,
     m_part, m_r0, m_h1, m_r1, m_h2, m_r2, m_r3, m_fin,
     g_part, g_r0, g_h1, g_r1, g_h2, g_r2, g_r3, g_fin,
-    xbuf, jbuf, rfac,
+    jbuf,
     lsem, ssem, rsem, csend, crecvs,
 ):
     x = lax.axis_index("tm")
@@ -129,7 +152,6 @@
         peers += [to_z(plus(z, d)), to_y(plus(y, d)), to_x(plus(x, d))]
     for peer in peers:
         pl.semaphore_signal(barrier, inc=1, device_id=peer, device_id_type=MESH)
-    pl.semaphore_wait(barrier, len(peers))
 
     def all_reduce(w, part, r0, h1, r1, h2, r2, r3, fin):
         base = al(core * 256, 256)
@@ -202,6 +224,8 @@
         fh[rows, :] = high
         fl[rows, :] = low
         part[rows, :] = mm3(fh[rows, :], fl[rows, :], rh[...], rl[...])
+        if n == 0:
+            pl.semaphore_wait(barrier, len(peers))
         if d:
             pcopies.append(send(part.at[rows], precv.at[d - 1], to_x(xx)))
 
@@ -328,8 +352,6 @@
     next(ar_g)
     for cp in scopies:
         cp.wait_recv()
-    outs = [pltpu.make_async_copy(sbuf, s_out, lsem.at[6])]
-    outs[0].start()
     gram = jnp.concatenate([g_fin[0:256, :], g_fin[256:512, :]], axis=1)
     for cp in x1:
         cp.wait_recv()
@@ -347,16 +369,10 @@
         forward.append(send(xbuf.at[yy, :, ra], xbuf.at[yy, :, ra], to_core()))
         forward.append(send(xbuf.at[:, zz, rb], xbuf.at[:, zz, rb], to_core()))
     inverse, upper = factor_second(*first)
-    jbuf2, rfac2 = jbuf, rfac
-    rfac2[0] = inverse
-    rfac2[1] = upper
+    j_out[...] = inverse
+    r_out[...] = upper
     for cp in forward:
         cp.wait_recv()
-    outs.append(pltpu.make_async_copy(xbuf, x_out, lsem.at[7]))
-    outs.append(pltpu.make_async_copy(rfac.at[0], j_out, lsem.at[8]))
-    outs.append(pltpu.make_async_copy(rfac.at[1], r_out, lsem.at[9]))
-    for copy in outs[1:]:
-        copy.start()
     for cp in sent:
         cp.wait_send()
 
@@ -365,8 +381,6 @@
         return carry
 
     lax.fori_loop(0, 8, drain, 0)
-    for copy in outs:
-        copy.wait()
 
 
 def last(scale, field, s, xb, inv, up, left, right, residual, sh, sl):
@@ -377,9 +391,11 @@
         sl[...] = low
 
     j = pl.program_id(0)
-    block = jnp.concatenate([xb[0], xb[1]], axis=1)
+    cols = pl.ds(pl.multiple_of(j * 256, 256), 256)
+    row, first = j // 2, lax.rem(j, 2) * 2
+    block = jnp.concatenate([xb[row, first], xb[row, first + 1]], axis=1)
     xh, xl = halves(block)
-    residual[...] = field[...] - mm3(sh[...], sl[...], xh, xl)
+    residual[...] = field[:, cols] - mm3(sh[...], sl[...], xh, xl)
     uh, ul = halves(up[...])
     right[...] = mm3(uh, ul, xh, xl)
     ih, il = halves(inv[...].T)
@@ -398,39 +414,34 @@
         ]
 
     any_space = pl.BlockSpec(memory_space=pl.ANY)
-    s, xb, inv, up = pl.pallas_call(
+    here = pl.BlockSpec(memory_space=pltpu.VMEM)
+    copy, s, xb, inv, up = pl.pallas_call(
         kernel,
-        out_shape=(
-            jax.ShapeDtypeStruct((1024, 256), F32),
-            jax.ShapeDtypeStruct((4, 4, 256, 128), F32),
-            jax.ShapeDtypeStruct((256, 256), F32),
-            jax.ShapeDtypeStruct((256, 256), F32),
-        ),
+        out_shape=(vm(1024, 2048), vm(1024, 256), vm(4, 4, 256, 128), vm(256, 256), vm(256, 256)),
         in_specs=[any_space] * 3,
-        out_specs=[any_space] * 4,
+        out_specs=[here] * 5,
         scratch_shapes=[
-            vm(1024, 2048), vm(2048, 256), vm(512, 1024),
+            vm(2048, 256), vm(512, 1024),
             vm(1024, 2048, dtype=BF16), vm(1024, 2048, dtype=BF16),
             vm(2048, 256, dtype=BF16), vm(2048, 256, dtype=BF16),
             vm(512, 1024, dtype=BF16), vm(512, 1024, dtype=BF16),
-            vm(1024, 256), vm(3, 256, 256), vm(1024, 256),
+            vm(1024, 256), vm(3, 256, 256),
             vm(4, 4, 512, 128), vm(4, 4, 256, 128),
             vm(3, 4, 128, 128), vm(3, 4, 128, 128), vm(4, 128, 128), vm(4, 128, 128),
             vm(3, 128, 128), vm(3, 128, 128), vm(512, 128),
             *reduce_buffers(256),
             *reduce_buffers(128),
-            vm(4, 4, 256, 128), vm(256, 128), vm(2, 256, 256),
-            pltpu.SemaphoreType.DMA((10,)),
+            vm(256, 128),
+            pltpu.SemaphoreType.DMA((6,)),
             pltpu.SemaphoreType.DMA((120,)),
             pltpu.SemaphoreType.DMA((120,)),
             pltpu.SemaphoreType.DMA((8,)),
             pltpu.SemaphoreType.DMA((8,)),
         ],
         compiler_params=pltpu.CompilerParams(
-            collective_id=0, has_side_effects=True, vmem_limit_bytes=64 * 1024 * 1024 - 65536),
+            collective_id=0, has_side_effects=True, vmem_limit_bytes=44 * 1024 * 1024),
         name="sketch",
     )(field, range_test, corange_test)
-    xb = xb.reshape(16, 256, 128)
     return pl.pallas_call(
         functools.partial(last, float(cells) ** 0.5),
         grid=(8,),
@@ -439,21 +450,16 @@
             jax.ShapeDtypeStruct((256, 2048), F32),
             jax.ShapeDtypeStruct((1024, 2048), F32),
         ),
-        in_specs=[
-            pl.BlockSpec((1024, 256), lambda j: (0, j)),
-            pl.BlockSpec((1024, 256), lambda j: (0, 0)),
-            pl.BlockSpec((2, 256, 128), lambda j: (j, 0, 0)),
-            pl.BlockSpec((256, 256), lambda j: (0, 0)),
-            pl.BlockSpec((256, 256), lambda j: (0, 0)),
-        ],
+        in_specs=[here] * 5,
         out_specs=(
             pl.BlockSpec((128, 256), lambda j: (j, 0)),
             pl.BlockSpec((256, 256), lambda j: (0, j)),
             pl.BlockSpec((1024, 256), lambda j: (0, j)),
         ),
         scratch_shapes=[vm(1024, 256, dtype=BF16), vm(1024, 256, dtype=BF16)],
+        compiler_params=pltpu.CompilerParams(vmem_limit_bytes=32 * 1024 * 1024),
         name="finish",
-    )(field, s, xb, inv, up)
+    )(copy, s, xb, inv, up)
 
 
 def solution(mesh):

time: 138 us -> 88.6 us (0.64)
  Pallas kernels: 137 us -> 87.9 us
    pallas_call x1, Pallas kernels: 124 us -> 79.9 us  [per_device(): pl.pallas_call(kernel, out_shape=(vm(1024, 2048), vm(1024, 256), vm(4, 4,...]
    pallas_call x1, Pallas kernels: 13 us -> 8.02 us  [per_device(): pl.pallas_call(functools.partial(last, float(cells) ** 0.5), grid=(8,), o...]
where the time goes in v1:
time: 88.6 us; the launch traced here: 88.5 us
  Pallas kernels  87.9 us (99%)
    pallas_call x1, Pallas kernels, per_device(): pl.pallas_call(kernel, out_shape=(vm(1024, 2048), vm(1024, 256), vm(4, 4,...  79.9 us
    pallas_call x1, Pallas kernels, per_device(): pl.pallas_call(functools.partial(last, float(cells) ** 0.5), grid=(8,), o...  8.02 us

profile of v1, /device:TPU:1, one launch (start us, length us, event | category | flops | bytes accessed | tf_op | source)
XLA Modules:
  0.0 88.5 jit_solution(7553749490168052198)
XLA Ops:
  0.6 79.9 %sketch.1 = (f32[1024,2048]{1,0:T(8,128)S(1)}, f32[1024,256]{1,0:T(8,128)S(1)}, f32[4,4,256,128]{3,2,1,0:T(8,128)S(1)}, f32[256,256]{1,0:T(8,128)S(1)}, f32[256,256]{1,0:T(8,128)S(1)}) custom-call(f32[1024,2048]{1,0:T(8,128)} %field.1, f32[2048,256]{1,0:T(8,128)} %rng.1, f32[512,1024]{1,0:T(8,128)} %cor.1), custom_call_target="tpu_custom_call" | custom-call | tf_op jit(solution)/shard_map/sketch/pallas_call | solution.py:418
  80.5 8.0 %finish.1 = (f32[1024,256]{1,0:T(8,128)}, f32[256,2048]{1,0:T(8,128)}, f32[1024,2048]{1,0:T(8,128)}) custom-call(f32[1024,2048]{1,0:T(8,128)S(1)} %get-tuple-element.8.field, f32[1024,256]{1,0:T(8,128)S(1)} %get-tuple-element.9.s, f32[4,4,256,128]{3,2,1,0:T(8,128)S(1)} %get-tuple-element.10.xb, f32[256,256]{1,0:T(8,128)S(1)} %get-tuple-element.11.inv, ...), custom_call_target="tpu_custom_call" | custom-call | tf_op jit(solution)/shard_map/finish/pallas_call | solution.py:445

commit v2 on v1

--- a/solution.py
+++ b/solution.py
@@ -29,7 +29,7 @@
     return jnp.dot(a, b, preferred_element_type=F32, precision=HI)
 
 
-def eliminate(matrix):
+def eliminate(matrix, between):
     lane = lax.broadcasted_iota(jnp.int32, (8, 128), 1)
     sub = lax.broadcasted_iota(jnp.int32, (8, 128), 0)
 
@@ -79,6 +79,7 @@
     carry = (jnp.zeros((8, 128), F32), *(matrix[8 * b : 8 * b + 8, :] for b in range(16)))
     for n, active in enumerate((15, 11, 7, 3)):
         carry = lax.fori_loop(4 * n, 4 * n + 4, functools.partial(group, active), carry)
+        between()
     full = jnp.concatenate(carry[1:], axis=0)
     r = lax.broadcasted_iota(jnp.int32, (128, 128), 0)
     c = lax.broadcasted_iota(jnp.int32, (128, 128), 1)
@@ -93,9 +94,9 @@
     field, rng, cor, fbuf, sbuf, xbuf, j_out, r_out,
     rbuf, obuf, fh, fl, rh, rl, oh, ol,
     part, precv,
-    cpart, crecv, c1a, c1b, h2a, h2b, c2a, c2b, cfin,
+    cpart, crecv, c1, s1, t1, o1, u2, s2, w2, cfin,
     m_part, m_r0, m_h1, m_r1, m_h2, m_r2, m_r3, m_fin,
-    g_part, g_r0, g_h1, g_r1, g_h2, g_r2, g_r3, g_fin,
+    g_part, g_r1, g_h2, g_r2, g_sw, g_swr, g_r3, g_fin,
     jbuf,
     lsem, ssem, rsem, csend, crecvs,
 ):
@@ -109,6 +110,9 @@
     def plus(v, d):
         return lax.rem(v + d, 4)
 
+    def flip(v, e):
+        return (v, v + 1 - 2 * lax.rem(v, 2), plus(v, 2), 3 - v)[e]
+
     def to_core():
         return {"space": sp + 1 - 2 * core}
 
@@ -209,6 +213,59 @@
         cp = send(fin.at[mine], fin.at[mine], to_core())
         yield
         cp.wait_recv()
+        yield
+
+    def all_reduce_late(part, r1, h2, r2, sw, swr, r3, fin):
+        cps = []
+        for d in (1, 2, 3):
+            zz, yy = plus(z, d), plus(y, d)
+            cps.append(send(part.at[pl.ds(al(64 * zz, 64), 64)], r1.at[0, d - 1], to_z(zz)))
+            cps.append(send(part.at[pl.ds(al(256 + 64 * yy, 64), 64)], r1.at[1, d - 1], to_y(yy)))
+        yield
+        for cp in cps:
+            cp.wait_recv()
+        for k, v in ((0, z), (1, y)):
+            h2[k] = (part[pl.ds(al(256 * k + 64 * v, 64), 64), :] + r1[k, 0]) + (r1[k, 1] + r1[k, 2])
+        cps = []
+        for d in (1, 2, 3):
+            zz, yy = plus(z, d), plus(y, d)
+            cps.append(send(h2.at[0, pl.ds(al(16 * yy, 16), 16)], r2.at[0, d - 1], to_y(yy)))
+            cps.append(send(h2.at[1, pl.ds(al(16 * zz, 16), 16)], r2.at[1, d - 1], to_z(zz)))
+        yield
+        for cp in cps:
+            cp.wait_recv()
+        for k, v in ((0, y), (1, z)):
+            sw[16 * k : 16 * k + 16, :] = (h2[k, pl.ds(al(16 * v, 16), 16), :] + r2[k, 0]) + (r2[k, 1] + r2[k, 2])
+        cp = send(sw, swr, to_core())
+        yield
+        cp.wait_recv()
+        r3[x] = sw[...] + swr[...]
+        cps = [send(r3.at[x], r3.at[x], to_x(plus(x, d))) for d in (1, 2, 3)]
+        yield
+        for cp in cps:
+            cp.wait_recv()
+        total = (r3[0] + r3[1]) + (r3[2] + r3[3])
+        a = al(64 * z, 64)
+        b = al(256 + 64 * y, 64)
+        a16 = pl.ds(al(a + 16 * y, 16), 16)
+        b16 = pl.ds(al(b + 16 * z, 16), 16)
+        fin[a16, :] = total[0:16]
+        fin[b16, :] = total[16:32]
+        cps = []
+        for d in (1, 2, 3):
+            cps.append(send(fin.at[a16], fin.at[a16], to_y(plus(y, d))))
+            cps.append(send(fin.at[b16], fin.at[b16], to_z(plus(z, d))))
+        yield
+        for cp in cps:
+            cp.wait_recv()
+        a64, b64 = pl.ds(a, 64), pl.ds(b, 64)
+        cps = []
+        for d in (1, 2, 3):
+            cps.append(send(fin.at[a64], fin.at[a64], to_z(plus(z, d))))
+            cps.append(send(fin.at[b64], fin.at[b64], to_y(plus(y, d))))
+        yield
+        for cp in cps:
+            cp.wait_recv()
         yield
 
     loads[0].wait()
@@ -242,69 +299,133 @@
     mine = pl.ds(al(core * 256, 256), 256)
 
     def core_copy(j):
-        yy, zz = j // 2, lax.rem(j, 2) * 2
-        pair = pl.ds(zz, 2)
         return pltpu.make_async_remote_copy(
-            src_ref=cpart.at[yy, pair, other], dst_ref=crecv.at[yy, pair],
+            src_ref=cpart.at[j, :, other], dst_ref=crecv.at[j],
             send_sem=csend.at[j], recv_sem=crecvs.at[j], device_id=to_core(), device_id_type=MESH)
 
     def cos_step(j, carry):
-        cols = pl.ds(al(j * 256, 256), 256)
-        block = mm3(oh[...], ol[...], fh[:, cols], fl[:, cols])
-        yy, zz = j // 2, lax.rem(j, 2) * 2
-        cpart[yy, zz] = block[:, :128]
-        cpart[yy, zz + 1] = block[:, 128:]
+        k = j // 2
+        yy = jnp.where(k == 0, flip(y, 2), jnp.where(k == 1, flip(y, 1), jnp.where(k == 2, flip(y, 3), y)))
+        even = lax.rem(j, 2) == 0
+        za = jnp.where(even, flip(z, 2), flip(z, 3))
+        zb = jnp.where(even, flip(z, 1), z)
+        ca = pl.ds(al((yy * 4 + za) * 128, 128), 128)
+        cb = pl.ds(al((yy * 4 + zb) * 128, 128), 128)
+        bh = jnp.concatenate([fh[:, ca], fh[:, cb]], axis=1)
+        bl = jnp.concatenate([fl[:, ca], fl[:, cb]], axis=1)
+        block = mm3(oh[...], ol[...], bh, bl)
+        cpart[j, 0] = block[:, :128]
+        cpart[j, 1] = block[:, 128:]
         core_copy(j).start()
         return carry
 
-    def cos_join(j, carry):
+    where = {}
+    for j in range(8):
+        for t, ez in enumerate((2, 1) if j % 2 == 0 else (3, 0)):
+            where[(2, 1, 3, 0)[j // 2], ez] = (j, t)
+
+    turns = ((1, 3), (3, 1))
+
+    def over(p, stage):
+        return (lambda e: to_z(flip(z, e))) if (p < 2) == (stage == 1) else (lambda e: to_y(flip(y, e)))
+
+    def block_of(p, along, across):
+        j, t = where[(across, along) if p < 2 else (along, across)]
+        return crecv[j, t, 64 * p : 64 * p + 64, :]
+
+    c_in = []
+
+    def cos_join(j):
         core_copy(j).wait_recv()
-        yy, zz = j // 2, lax.rem(j, 2) * 2
-        pair = pl.ds(zz, 2)
-        crecv[yy, pair] = crecv[yy, pair] + cpart[yy, pair, mine]
-        return carry
+        crecv[j] = crecv[j] + cpart[j, :, mine]
+        for (ey, ez), (jj, t) in where.items():
+            if jj != j:
+                continue
+            for p in range(4):
+                along, across = (ez, ey) if p < 2 else (ey, ez)
+                near = turns[p % 2][0]
+                if along in (near, 2):
+                    c_in.append(send(
+                        crecv.at[j, t, 64 * p : 64 * p + 64], c1.at[p, int(along == 2), across], over(p, 1)(near)))
+
+    def take(copies):
+        for cp in copies:
+            cp.wait_recv()
+        del copies[:]
+
+    def c_1b():
+        take(c_in)
+        for p in range(4):
+            far = turns[p % 2][1]
+            for n in range(4):
+                s1[p, n] = block_of(p, far, n) + c1[p, 1, n]
+            c_in.append(send(s1.at[p], t1.at[p], over(p, 1)(far)))
+
+    def c_2a():
+        take(c_in)
+        for p in range(4):
+            for n in range(4):
+                o1[p, n] = (block_of(p, 0, n) + c1[p, 0, n]) + t1[p, n]
+            near = turns[p % 2][0]
+            lo = 1 if near == 1 else 2
+            c_in.append(send(o1.at[p, lo : lo + 2], u2.at[p], over(p, 2)(near)))
+
+    def c_2b():
+        take(c_in)
+        for p in range(4):
+            near, far = turns[p % 2]
+            s2[p] = o1[p, far] + u2[p, 1 if near == 1 else 0]
+            c_in.append(send(s2.at[p], w2.at[p], over(p, 2)(far)))
+
+    def c_end():
+        take(c_in)
+        for p in range(4):
+            near = turns[p % 2][0]
+            rows = pl.ds(al(core * 256 + 64 * p, 64), 64)
+            cfin[rows, :] = (o1[p, 0] + u2[p, 0 if near == 1 else 1]) + w2[p]
+        return send(cfin.at[mine], cfin.at[mine], to_core())
 
     lax.fori_loop(0, 2, cos_step, 0)
     next(ar_m)
-    lax.fori_loop(2, 4, cos_step, 0)
-    next(ar_m)
-    lax.fori_loop(4, 6, cos_step, 0)
+    lax.fori_loop(2, 6, cos_step, 0)
+    next(ar_m)
+    cos_join(0)
+    cos_join(1)
+    lax.fori_loop(6, 8, cos_step, 0)
     next(ar_m)
     for cp in pcopies:
         cp.wait_recv()
     own = pl.ds(al(x * 256, 256), 256)
     rows_sum = (part[own, :] + precv[0]) + (precv[1] + precv[2])
     sbuf[own, :] = rows_sum
-    scopies = [send(sbuf.at[own], sbuf.at[own], to_x(plus(x, d))) for d in (1, 2, 3)]
     gram = exact(rows_sum.T, rows_sum)
     g_part[0:256, :] = gram[:, :128]
     g_part[256:512, :] = gram[:, 128:]
-    ar_g = all_reduce(128, g_part, g_r0, g_h1, g_r1, g_h2, g_r2, g_r3, g_fin)
+    ar_g = all_reduce_late(g_part, g_r1, g_h2, g_r2, g_sw, g_swr, g_r3, g_fin)
+    cos_join(2)
+    cos_join(3)
+    next(ar_m)
     next(ar_g)
-    next(ar_m)
-    lax.fori_loop(6, 8, cos_step, 0)
+    cos_join(4)
+    cos_join(5)
+    next(ar_m)
+    scopies = [send(sbuf.at[own], sbuf.at[own], to_x(plus(x, d))) for d in (1, 2, 3)]
+    cos_join(6)
+    cos_join(7)
+    next(ar_m)
     next(ar_g)
-    next(ar_m)
-    lax.fori_loop(0, 8, cos_join, 0)
-    c1 = []
-    for d in (1, 2, 3):
-        zz, yy = plus(z, d), plus(y, d)
-        c1.append(send(crecv.at[:, zz, 0:128], c1a.at[d - 1], to_z(zz)))
-        c1.append(send(crecv.at[yy, :, 128:256], c1b.at[d - 1], to_y(yy)))
-    next(ar_g)
-    next(ar_m)
     next(ar_m)
     mixed = m_fin[...]
     mixed_t = mixed.T
     normal = exact(mixed_t, mixed)
 
-    def factor_first(a):
-        up, lo = eliminate(a[:128, :128])
+    def factor_first(a, between):
+        up, lo = eliminate(a[:128, :128], between)
         off = exact(lo, a[:128, 128:])
         return up, lo, off, a[128:, 128:] - exact(off.T, off)
 
-    def factor_second(up, lo, off, rest):
-        up2, lo2 = eliminate(rest)
+    def factor_second(up, lo, off, rest, between):
+        up2, lo2 = eliminate(rest, between)
         corner = -exact(lo2, exact(off.T, lo))
         zero = jnp.zeros((128, 128), F32)
         left = jnp.concatenate([lo, corner], axis=0)
@@ -314,28 +435,26 @@
         bottom = jnp.concatenate([zero, up2], axis=1)
         return inv, jnp.concatenate([top, bottom], axis=0)
 
-    next(ar_g)
-    first = factor_first(normal)
-    next(ar_g)
-    for cp in c1:
-        cp.wait_recv()
-    for n in range(4):
-        h2a[n] = (crecv[n, z, 0:128, :] + c1a[0, n]) + (c1a[1, n] + c1a[2, n])
-        h2b[n] = (crecv[y, n, 128:256, :] + c1b[0, n]) + (c1b[1, n] + c1b[2, n])
-    c2 = []
-    for d in (1, 2, 3):
-        zz, yy = plus(z, d), plus(y, d)
-        c2.append(send(h2a.at[yy], c2a.at[d - 1], to_y(yy)))
-        c2.append(send(h2b.at[zz], c2b.at[d - 1], to_z(zz)))
-    inverse, unused = factor_second(*first)
-    next(ar_g)
-    for cp in c2:
-        cp.wait_recv()
-    cbase = al(core * 256, 256)
-    cfin[pl.ds(cbase, 128), :] = (h2a[y] + c2a[0]) + (c2a[1] + c2a[2])
-    cfin[pl.ds(al(cbase + 128, 128), 128), :] = (h2b[z] + c2b[0]) + (c2b[1] + c2b[2])
-    cc = send(cfin.at[mine], cfin.at[mine], to_core())
+    def queue(*steps):
+        steps = list(steps)
+
+        def run():
+            if steps:
+                steps.pop(0)()
+
+        return run
+
+    def step_g():
+        next(ar_g)
+
+    def rest():
+        pass
+
+    c_1b()
+    first = factor_first(normal, queue(rest, step_g, step_g, c_2a))
+    inverse, unused = factor_second(*first, queue(step_g, rest, c_2b, step_g))
     solve = exact(inverse.T, exact(inverse, mixed_t))
+    cc = c_end()
     cc.wait_recv()
     block = exact(solve, cfin[...])
     half = al(core * 128, 128)
@@ -349,26 +468,47 @@
         x1.append(send(xbuf.at[y, z, ra], xbuf.at[y, z, ra], to_z(plus(z, d))))
         x1.append(send(xbuf.at[y, z, rb], xbuf.at[y, z, rb], to_y(plus(y, d))))
     next(ar_g)
-    next(ar_g)
     for cp in scopies:
         cp.wait_recv()
     gram = jnp.concatenate([g_fin[0:256, :], g_fin[256:512, :]], axis=1)
-    for cp in x1:
-        cp.wait_recv()
-    x2, forward = [], []
-    for d in (1, 2, 3):
-        x2.append(send(xbuf.at[y, :, ra], xbuf.at[y, :, ra], to_y(plus(y, d))))
-        x2.append(send(xbuf.at[:, z, rb], xbuf.at[:, z, rb], to_z(plus(z, d))))
-    forward.append(send(xbuf.at[y, :, ra], xbuf.at[y, :, ra], to_core()))
-    forward.append(send(xbuf.at[:, z, rb], xbuf.at[:, z, rb], to_core()))
-    first = factor_first(gram)
-    for d, (ca, cb) in zip((1, 2, 3), zip(x2[0::2], x2[1::2])):
-        ca.wait_recv()
-        cb.wait_recv()
-        yy, zz = plus(y, 4 - d), plus(z, 4 - d)
-        forward.append(send(xbuf.at[yy, :, ra], xbuf.at[yy, :, ra], to_core()))
-        forward.append(send(xbuf.at[:, zz, rb], xbuf.at[:, zz, rb], to_core()))
-    inverse, upper = factor_second(*first)
+
+    forward = []
+
+    def lot(p, e):
+        rows = pl.ds(al(half + 32 * p, 32), 32)
+        return xbuf.at[flip(y, e), :, rows] if p < 2 else xbuf.at[:, flip(z, e), rows]
+
+    def x_2a():
+        take(x1)
+        for p in range(4):
+            x1.append(send(lot(p, 0), lot(p, 0), over(p, 2)(turns[p % 2][1])))
+        for p in range(4):
+            forward.append(send(lot(p, 0), lot(p, 0), to_core()))
+
+    x_last = []
+
+    def x_2b():
+        for p in range(4):
+            near = turns[p % 2][0]
+            x_last.append(send(lot(p, 0), lot(p, 0), over(p, 2)(near)))
+        take(x1)
+        for p in range(4):
+            near, far = turns[p % 2]
+            x_last.append(send(lot(p, far), lot(p, far), over(p, 2)(near)))
+        for p in range(4):
+            far = turns[p % 2][1]
+            forward.append(send(lot(p, far), lot(p, far), to_core()))
+
+    def x_end(part):
+        for p in range(4):
+            near, far = turns[p % 2]
+            x_last[4 * part + p].wait_recv()
+            e = near if part == 0 else 2
+            forward.append(send(lot(p, e), lot(p, e), to_core()))
+
+    first = factor_first(gram, queue(rest, rest, x_2a))
+    inverse, upper = factor_second(*first, queue(x_2b, rest, rest, lambda: x_end(0)))
+    x_end(1)
     j_out[...] = inverse
     r_out[...] = upper
     for cp in forward:
@@ -426,15 +566,16 @@
             vm(2048, 256, dtype=BF16), vm(2048, 256, dtype=BF16),
             vm(512, 1024, dtype=BF16), vm(512, 1024, dtype=BF16),
             vm(1024, 256), vm(3, 256, 256),
-            vm(4, 4, 512, 128), vm(4, 4, 256, 128),
-            vm(3, 4, 128, 128), vm(3, 4, 128, 128), vm(4, 128, 128), vm(4, 128, 128),
-            vm(3, 128, 128), vm(3, 128, 128), vm(512, 128),
+            vm(8, 2, 512, 128), vm(8, 2, 256, 128),
+            vm(4, 2, 4, 64, 128), vm(4, 4, 64, 128), vm(4, 4, 64, 128), vm(4, 4, 64, 128),
+            vm(4, 2, 64, 128), vm(4, 64, 128), vm(4, 64, 128), vm(512, 128),
             *reduce_buffers(256),
-            *reduce_buffers(128),
+            vm(512, 128), vm(2, 3, 64, 128), vm(2, 64, 128), vm(2, 3, 16, 128),
+            vm(32, 128), vm(32, 128), vm(4, 32, 128), vm(512, 128),
             vm(256, 128),
             pltpu.SemaphoreType.DMA((6,)),
-            pltpu.SemaphoreType.DMA((120,)),
-            pltpu.SemaphoreType.DMA((120,)),
+            pltpu.SemaphoreType.DMA((180,)),
+            pltpu.SemaphoreType.DMA((180,)),
             pltpu.SemaphoreType.DMA((8,)),
             pltpu.SemaphoreType.DMA((8,)),
         ],

time: 88.6 us -> 80.9 us (0.913)
  Pallas kernels: 87.9 us -> 80.2 us
    pallas_call x1, Pallas kernels: 79.9 us -> 72.1 us  [per_device(): pl.pallas_call(kernel, out_shape=(vm(1024, 2048), vm(1024, 256), vm(4, 4,...]
where the time goes in v2:
time: 80.9 us; the launch traced here: 80.8 us
  Pallas kernels  80.2 us (99%)
    pallas_call x1, Pallas kernels, per_device(): pl.pallas_call(kernel, out_shape=(vm(1024, 2048), vm(1024, 256), vm(4, 4,...  72.1 us
    pallas_call x1, Pallas kernels, per_device(): pl.pallas_call(functools.partial(last, float(cells) ** 0.5), grid=(8,), o...  8.02 us

profile of v2, /device:TPU:1, one launch (start us, length us, event | category | flops | bytes accessed | tf_op | source)
XLA Modules:
  0.0 80.8 jit_solution(8748354059068029966)
XLA Ops:
  0.6 72.1 %sketch.1 = (f32[1024,2048]{1,0:T(8,128)S(1)}, f32[1024,256]{1,0:T(8,128)S(1)}, f32[4,4,256,128]{3,2,1,0:T(8,128)S(1)}, f32[256,256]{1,0:T(8,128)S(1)}, f32[256,256]{1,0:T(8,128)S(1)}) custom-call(f32[1024,2048]{1,0:T(8,128)} %field.1, f32[2048,256]{1,0:T(8,128)} %rng.1, f32[512,1024]{1,0:T(8,128)} %cor.1), custom_call_target="tpu_custom_call" | custom-call | tf_op jit(solution)/shard_map/sketch/pallas_call | solution.py:558
  72.8 8.0 %finish.1 = (f32[1024,256]{1,0:T(8,128)}, f32[256,2048]{1,0:T(8,128)}, f32[1024,2048]{1,0:T(8,128)}) custom-call(f32[1024,2048]{1,0:T(8,128)S(1)} %get-tuple-element.8.field, f32[1024,256]{1,0:T(8,128)S(1)} %get-tuple-element.9.s, f32[4,4,256,128]{3,2,1,0:T(8,128)S(1)} %get-tuple-element.10.xb, f32[256,256]{1,0:T(8,128)S(1)} %get-tuple-element.11.inv, ...), custom_call_target="tpu_custom_call" | custom-call | tf_op jit(solution)/shard_map/finish/pallas_call | solution.py:586

commit v3 on v2

--- a/solution.py
+++ b/solution.py
@@ -280,7 +280,7 @@
         high, low = halves(fbuf[rows, :])
         fh[rows, :] = high
         fl[rows, :] = low
-        part[rows, :] = mm3(fh[rows, :], fl[rows, :], rh[...], rl[...])
+        part[rows, :] = mm3(high, low, rh[...], rl[...])
         if n == 0:
             pl.semaphore_wait(barrier, len(peers))
         if d:
@@ -523,12 +523,18 @@
     lax.fori_loop(0, 8, drain, 0)
 
 
-def last(scale, field, s, xb, inv, up, left, right, residual, sh, sl):
+def last(scale, field, s, xb, inv, up, left, right, residual, sh, sl, ih, il, uh, ul):
     @pl.when(pl.program_id(0) == 0)
     def _():
         high, low = halves(s[...])
         sh[...] = high
         sl[...] = low
+        high, low = halves(inv[...].T)
+        ih[...] = high
+        il[...] = low
+        high, low = halves(up[...])
+        uh[...] = high
+        ul[...] = low
 
     j = pl.program_id(0)
     cols = pl.ds(pl.multiple_of(j * 256, 256), 256)
@@ -536,11 +542,9 @@
     block = jnp.concatenate([xb[row, first], xb[row, first + 1]], axis=1)
     xh, xl = halves(block)
     residual[...] = field[:, cols] - mm3(sh[...], sl[...], xh, xl)
-    uh, ul = halves(up[...])
-    right[...] = mm3(uh, ul, xh, xl)
-    ih, il = halves(inv[...].T)
+    right[...] = mm3(uh[...], ul[...], xh, xl)
     rows = pl.ds(pl.multiple_of(j * 128, 128), 128)
-    left[...] = mm3(sh[rows, :], sl[rows, :], ih, il) * scale
+    left[...] = mm3(sh[rows, :], sl[rows, :], ih[...], il[...]) * scale
 
 
 def per_device(cells, field, range_test, corange_test):
@@ -597,7 +601,7 @@
             pl.BlockSpec((256, 256), lambda j: (0, j)),
             pl.BlockSpec((1024, 256), lambda j: (0, j)),
         ),
-        scratch_shapes=[vm(1024, 256, dtype=BF16), vm(1024, 256, dtype=BF16)],
+        scratch_shapes=[vm(1024, 256, dtype=BF16)] * 2 + [vm(256, 256, dtype=BF16)] * 4,
         compiler_params=pltpu.CompilerParams(vmem_limit_bytes=32 * 1024 * 1024),
         name="finish",
     )(copy, s, xb, inv, up)

time: 80.9 us -> 81.3 us (level)
  no operation moved by 1% of the time
where the time goes in v3:
time: 81.3 us; the launch traced here: 81.2 us
  Pallas kernels  80.6 us (99%)
    pallas_call x1, Pallas kernels, per_device(): pl.pallas_call(kernel, out_shape=(vm(1024, 2048), vm(1024, 256), vm(4, 4,...  72.2 us
    pallas_call x1, Pallas kernels, per_device(): pl.pallas_call(functools.partial(last, float(cells) ** 0.5), grid=(8,), o...  8.34 us

profile of v3, /device:TPU:1, one launch (start us, length us, event | category | flops | bytes accessed | tf_op | source)
XLA Modules:
  0.0 81.2 jit_solution(10194768380000189550)
XLA Ops:
  0.6 72.2 %sketch.1 = (f32[1024,2048]{1,0:T(8,128)S(1)}, f32[1024,256]{1,0:T(8,128)S(1)}, f32[4,4,256,128]{3,2,1,0:T(8,128)S(1)}, f32[256,256]{1,0:T(8,128)S(1)}, f32[256,256]{1,0:T(8,128)S(1)}) custom-call(f32[1024,2048]{1,0:T(8,128)} %field.1, f32[2048,256]{1,0:T(8,128)} %rng.1, f32[512,1024]{1,0:T(8,128)} %cor.1), custom_call_target="tpu_custom_call" | custom-call | tf_op jit(solution)/shard_map/sketch/pallas_call | solution.py:562
  72.9 8.3 %finish.1 = (f32[1024,256]{1,0:T(8,128)}, f32[256,2048]{1,0:T(8,128)}, f32[1024,2048]{1,0:T(8,128)}) custom-call(f32[1024,2048]{1,0:T(8,128)S(1)} %get-tuple-element.8.field, f32[1024,256]{1,0:T(8,128)S(1)} %get-tuple-element.9.s, f32[4,4,256,128]{3,2,1,0:T(8,128)S(1)} %get-tuple-element.10.xb, f32[256,256]{1,0:T(8,128)S(1)} %get-tuple-element.11.inv, ...), custom_call_target="tpu_custom_call" | custom-call | tf_op jit(solution)/shard_map/finish/pallas_call | solution.py:590
